TPU v7x, 32 devices: a whole 2x2x4 slice. The times are simulated.
32 devices in a mesh: rows: 8 (over z, y), sub: 4 (over x, core).
Axes of the slice: x: 2, y: 2, z: 4, core: 2. Of those that a mesh axis runs over, the one named last changes fastest.
Arguments:
- embeddings: bfloat16 [16384, 768], P(('rows', 'sub')), may hold values from -0.25 to 0.25
- factor: float32 [16384, 512], P(('rows', 'sub')), may hold values from -0.15 to 0.15
- diagonal: float32 [16384], P(('rows', 'sub')), may hold values from 0.5 to 1
- pivot_owner: int32 [4, 256], replicated, may hold values from 0 to 31, as said below
- pivot_local: int32 [4, 256], replicated, may hold values from 0 to 511, as said below
Outputs:
- new_columns: float32 [16384, 1024], P(('rows', 'sub'))
- new_diagonal: float32 [16384], P(('rows', 'sub'))
Inputs may be any that keep to these rules, and one draw needn't show every extreme that they name: The 1024 global rows pivot_owner * 512 + pivot_local are all different; row 0 and the last row of all are among them. `pivot_local`: read together with pivot_owner.
All inputs are finite; a program needn't handle non-finite values.
Results may differ from a plain program's by a relative error of at most 0.0003.
Values sent between devices are 32-bit elements; how exact they have to be, the bound alone decides.
No kernel may reach another device: no remote copies, remote signals or barrier semaphores. Data moves between devices by JAX's collectives and lax.ppermute only.
A program may use at most 64 MiB of HBM per device.

v0:
```python
import jax
import jax.numpy as jnp
from jax import lax
from jax.sharding import PartitionSpec as P

gamma_scale = 1.0
ridge_base = 0.5


def gauss_kernel(left, left_squares, right, right_squares):
    inner = jnp.dot(left, right.T, preferred_element_type=jnp.float32)
    return jnp.exp(-gamma_scale * (left_squares[:, None] + right_squares[None, :] - 2.0 * inner))


def gershgorin(pivot_gram):
    absolute = jnp.sum(jnp.abs(pivot_gram), axis=1) - jnp.abs(jnp.diagonal(pivot_gram))
    return ridge_base + jnp.maximum(jnp.max(absolute - jnp.diagonal(pivot_gram)), 0.0)


def selector(owners, locals_row, device, local_rows):
    positions = lax.broadcasted_iota(jnp.int32, (owners.shape[0], local_rows), 1)
    hits = (owners[:, None] == device) & (locals_row[:, None] == positions)
    return hits.astype(jnp.float32)


def on_device(embeddings, factor, diagonal, pivot_owner, pivot_local):
    local_rows = embeddings.shape[0]
    pivots = pivot_owner.shape[1]
    blocks = pivot_owner.shape[0]
    device = lax.axis_index("rows") * lax.axis_size("sub") + lax.axis_index("sub")
    squares = jnp.sum(jnp.square(embeddings.astype(jnp.float32)), axis=1)
    identity = jnp.eye(pivots, dtype=jnp.float32)
    columns = factor
    residual_diag = diagonal
    blocks_out = []
    later_rows = [[] for block in range(blocks)]
    select_all = selector(pivot_owner.reshape(-1), pivot_local.reshape(-1), device, local_rows)
    all_points = jnp.dot(
        select_all.astype(jnp.bfloat16), embeddings, preferred_element_type=jnp.float32
    )
    all_factor = jnp.dot(select_all, factor, precision=lax.Precision.HIGHEST)
    all_points, all_factor = lax.psum((all_points, all_factor), ("rows", "sub"))
    for block in range(blocks):
        point_rows = all_points[block * pivots : (block + 1) * pivots]
        factor_rows = jnp.concatenate(
            [all_factor[block * pivots : (block + 1) * pivots]] + later_rows[block], axis=1
        )
        points = point_rows.astype(jnp.bfloat16)
        point_squares = jnp.sum(point_rows * point_rows, axis=1)
        kernel = gauss_kernel(embeddings, squares, points, point_squares)
        resid = kernel - jnp.dot(columns, factor_rows.T, precision=lax.Precision.HIGHEST)
        pivot_kernel = gauss_kernel(points, point_squares, points, point_squares)
        pivot_gram = pivot_kernel - jnp.dot(
            factor_rows, factor_rows.T, precision=lax.Precision.HIGHEST
        )
        pivot_gram = 0.5 * (pivot_gram + pivot_gram.T)
        shift = gershgorin(pivot_gram)
        lower = jnp.linalg.cholesky(pivot_gram + shift * identity)
        inverse = lax.linalg.triangular_solve(lower, identity, left_side=True, lower=True)
        block_cols = jnp.dot(resid, inverse.T, precision=lax.Precision.HIGHEST)
        residual_diag = residual_diag - jnp.sum(block_cols * block_cols, axis=1)
        columns = jnp.concatenate([columns, block_cols], axis=1)
        blocks_out.append(block_cols)
        for later in range(block + 1, blocks):
            later_rows_f = all_points[later * pivots : (later + 1) * pivots]
            later_points = later_rows_f.astype(jnp.bfloat16)
            later_squares = jnp.sum(later_rows_f * later_rows_f, axis=1)
            later_cols = jnp.concatenate(
                [all_factor[later * pivots : (later + 1) * pivots]] + later_rows[later], axis=1
            )
            cross = gauss_kernel(later_points, later_squares, points, point_squares)
            cross = cross - jnp.dot(later_cols, factor_rows.T, precision=lax.Precision.HIGHEST)
            later_rows[later].append(jnp.dot(cross, inverse.T, precision=lax.Precision.HIGHEST))
    return (jnp.concatenate(blocks_out, axis=1), residual_diag)


def solution(mesh):
    return jax.shard_map(
        on_device,
        mesh=mesh,
        in_specs=(P(("rows", "sub"), None), P(("rows", "sub"), None), P(("rows", "sub")), P(), P()),
        out_specs=(P(("rows", "sub"), None), P(("rows", "sub"))),
        check_vma=False,
    )
```

profile of v0, /device:TPU:0, one launch (start us, length us, event | category | flops | bytes accessed | tf_op | source)
XLA Modules:
  0.0 617.7 jit_solution(4231253984314557761)
XLA Ops:
  8.6 3.9 fusion.62
  17.6 149.4 %all-reduce.4.cloned.1.call-done = (f32[1024,768]{1,0:T(8,128)}, f32[1024,512]{1,0:T(8,128)}) async-done(((f32[1024,768]{1,0:T(8,128)}, f32[1024,512]{1,0:T(8,128)}), (f32[1024,768]{1,0:T(8,128)}, f32[1024,512]{1,0:T(8,128)})) %all-reduce.4.cloned.1.call-update) | async-done | bytes 5242896 | tf_op jit(solution)/shard_map/psum | solution.py:42
  197.8 11.7 %cholesky.214 = f32[128,128]{1,0:T(8,128)S(1)} custom-call(f32[128,128]{1,0:T(8,128)S(1)} %copy.79), custom_call_target="Cholesky" | custom-call | tf_op jit(solution)/shard_map/jit(cholesky)/cholesky | solution.py:58
  212.1 11.3 %custom-call.25 = f32[1,128,128]{1,2,0:T(8,128)} custom-call(f32[1,128,128]{2,1,0:T(8,128)} %get-tuple-element.114), custom_call_target="InvertDiagBlocksLowerTriangular" | custom-call | tf_op jit(solution)/shard_map/jit(cholesky)/cholesky | solution.py:58
  227.8 13.2 %cholesky.231 = f32[128,128]{1,0:T(8,128)} custom-call(f32[128,128]{1,0:T(8,128)} %copy.81), custom_call_target="Cholesky" | custom-call | tf_op jit(solution)/shard_map/jit(cholesky)/cholesky | solution.py:58
  247.4 6.6 %while.8 = (s32[]{:T(128)}, f32[256,256]{1,0:T(8,128)S(1)}, s32[2,2]{1,0:T(2,128)}, f32[2,128,128]{2,1,0:T(8,128)}, s32[]{:T(128)}) while((s32[]{:T(128)}, f32[256,256]{1,0:T(8,128)S(1)}, s32[2,2]{1,0:T(2,128)}, f32[2,128,128]{2,1,0:T(8,128)}, s32[]{:T(128)}) %tuple.103), condition=%wide.while_cond, body=%wide.while_body.sunk | while | flops 2 | bytes 132705 | solution.py:59
  254.0 21.3 %custom-call.26 = f32[2,128,128]{1,2,0:T(8,128)} custom-call(f32[2,128,128]{2,1,0:T(8,128)} %get-tuple-element.30), custom_call_target="InvertDiagBlocksLowerTriangular" | custom-call | tf_op jit(solution)/shard_map/triangular_solve/custom-call.0 | solution.py:59
  298.6 11.7 %cholesky.248 = f32[128,128]{1,0:T(8,128)S(1)} custom-call(f32[128,128]{1,0:T(8,128)S(1)} %copy.92), custom_call_target="Cholesky" | custom-call | tf_op jit(solution)/shard_map/jit(cholesky)/cholesky | solution.py:58
  313.0 11.3 %custom-call.27 = f32[1,128,128]{1,2,0:T(8,128)} custom-call(f32[1,128,128]{2,1,0:T(8,128)} %get-tuple-element.110), custom_call_target="InvertDiagBlocksLowerTriangular" | custom-call | tf_op jit(solution)/shard_map/jit(cholesky)/cholesky | solution.py:58
  328.7 13.2 %cholesky.265 = f32[128,128]{1,0:T(8,128)} custom-call(f32[128,128]{1,0:T(8,128)} %copy.94), custom_call_target="Cholesky" | custom-call | tf_op jit(solution)/shard_map/jit(cholesky)/cholesky | solution.py:58
  347.5 8.5 %while.9 = (s32[]{:T(128)}, f32[256,256]{1,0:T(8,128)}, s32[2,2]{1,0:T(2,128)}, f32[2,128,128]{2,1,0:T(8,128)}, s32[]{:T(128)}) while((s32[]{:T(128)}, f32[256,256]{1,0:T(8,128)}, s32[2,2]{1,0:T(2,128)}, f32[2,128,128]{2,1,0:T(8,128)}, s32[]{:T(128)}) %tuple.118), condition=%wide.while_cond.clone, body=%wide.while_body.clone.sunk | while | flops 2 | bytes 132705 | solution.py:59
  356.0 21.2 %custom-call.28 = f32[2,128,128]{1,2,0:T(8,128)} custom-call(f32[2,128,128]{2,1,0:T(8,128)} %get-tuple-element.31), custom_call_target="InvertDiagBlocksLowerTriangular" | custom-call | tf_op jit(solution)/shard_map/triangular_solve/custom-call.0 | solution.py:59
  406.2 11.7 %cholesky.282 = f32[128,128]{1,0:T(8,128)S(1)} custom-call(f32[128,128]{1,0:T(8,128)S(1)} %cholesky.352), custom_call_target="Cholesky" | custom-call | tf_op jit(solution)/shard_map/jit(cholesky)/cholesky | solution.py:58
  420.5 11.3 %custom-call.29 = f32[1,128,128]{1,2,0:T(8,128)} custom-call(f32[1,128,128]{2,1,0:T(8,128)} %get-tuple-element.106), custom_call_target="InvertDiagBlocksLowerTriangular" | custom-call | tf_op jit(solution)/shard_map/jit(cholesky)/cholesky | solution.py:58
  434.6 13.2 %cholesky.299 = f32[128,128]{1,0:T(8,128)} custom-call(f32[128,128]{1,0:T(8,128)} %convolution_subtract_fusion.10), custom_call_target="Cholesky" | custom-call | tf_op jit(solution)/shard_map/jit(cholesky)/cholesky | solution.py:58
  453.4 6.3 %while.10 = (s32[]{:T(128)}, f32[256,256]{1,0:T(8,128)S(1)}, s32[2,2]{1,0:T(2,128)}, f32[2,128,128]{2,1,0:T(8,128)}, s32[]{:T(128)}) while((s32[]{:T(128)}, f32[256,256]{1,0:T(8,128)S(1)}, s32[2,2]{1,0:T(2,128)}, f32[2,128,128]{2,1,0:T(8,128)}, s32[]{:T(128)}) %tuple.119), condition=%wide.while_cond.clone.1, body=%wide.while_body.clone.1.sunk | while | flops 2 | bytes 132705 | solution.py:59
  459.7 21.1 %custom-call.30 = f32[2,128,128]{1,2,0:T(8,128)} custom-call(f32[2,128,128]{2,1,0:T(8,128)} %get-tuple-element.32), custom_call_target="InvertDiagBlocksLowerTriangular" | custom-call | tf_op jit(solution)/shard_map/triangular_solve/custom-call.0 | solution.py:59
  486.2 3.5 fusion.79
  505.3 11.7 %cholesky.316 = f32[128,128]{1,0:T(8,128)S(1)} custom-call(f32[128,128]{1,0:T(8,128)S(1)} %cholesky.355), custom_call_target="Cholesky" | custom-call | tf_op jit(solution)/shard_map/jit(cholesky)/cholesky | solution.py:58
  519.1 11.3 %custom-call.31 = f32[1,128,128]{1,2,0:T(8,128)} custom-call(f32[1,128,128]{2,1,0:T(8,128)} %get-tuple-element.102), custom_call_target="InvertDiagBlocksLowerTriangular" | custom-call | tf_op jit(solution)/shard_map/jit(cholesky)/cholesky | solution.py:58
  533.2 13.2 %cholesky.333 = f32[128,128]{1,0:T(8,128)} custom-call(f32[128,128]{1,0:T(8,128)} %convolution_subtract_fusion.9), custom_call_target="Cholesky" | custom-call | tf_op jit(solution)/shard_map/jit(cholesky)/cholesky | solution.py:58
  551.2 8.3 %while.11 = (s32[]{:T(128)}, f32[256,256]{1,0:T(8,128)}, s32[2,2]{1,0:T(2,128)}, f32[2,128,128]{2,1,0:T(8,128)}, s32[]{:T(128)}) while((s32[]{:T(128)}, f32[256,256]{1,0:T(8,128)}, s32[2,2]{1,0:T(2,128)}, f32[2,128,128]{2,1,0:T(8,128)}, s32[]{:T(128)}) %tuple.120), condition=%wide.while_cond.clone.2, body=%wide.while_body.clone.2.sunk | while | flops 2 | bytes 132705 | solution.py:59
  559.5 21.3 %custom-call.32 = f32[2,128,128]{1,2,0:T(8,128)} custom-call(f32[2,128,128]{2,1,0:T(8,128)} %get-tuple-element.33), custom_call_target="InvertDiagBlocksLowerTriangular" | custom-call | tf_op jit(solution)/shard_map/triangular_solve/custom-call.0 | solution.py:59
  601.3 4.0 fusion
  (294 shorter events, 204.7 us)
Async XLA Ops:
  7.2 159.8 %all-reduce.4.cloned.1.call-start = ((), (), s32[]{:S(2)}) async-start(), calls=%async_computation | async-start | bytes 10485760 | tf_op jit(solution)/shard_map/psum | solution.py:42
  8.6 3.9 copy-start.1
  169.8 5.8 copy-start.10
  169.8 10.2 %copy-start.12 = (bf16[256,768]{1,0:T(8,128)(2,1)}, bf16[256,768]{1,0:T(8,128)(2,1)S(1)}, u32[]{:S(2)}) copy-start(bf16[256,768]{1,0:T(8,128)(2,1)S(1)} %get-tuple-element.93) | copy-start | bytes 1179652
  170.1 9.9 %copy-start.57 = (f32[256]{0:T(256)}, f32[256]{0:T(256)S(1)}, u32[]{:S(2)}) copy-start(f32[256]{0:T(256)S(1)} %get-tuple-element.39) | copy-start | bytes 3076
  170.4 12.0 %copy-start.25 = (f32[256,256]{0,1:T(8,128)}, f32[256,256]{0,1:T(8,128)S(1)}, u32[]{:S(2)}) copy-start(f32[256,256]{0,1:T(8,128)S(1)} %convolution_multiply_fusion.13) | copy-start | bytes 786436
  275.3 4.3 copy-start.54
  276.5 4.8 copy-start.14
  347.5 35.4 %copy-start.8 = (f32[256,256]{1,0:T(8,128)S(1)}, f32[256,256]{1,0:T(8,128)}, u32[]{:S(2)}) copy-start(f32[256,256]{1,0:T(8,128)} %copy-done.7) | copy-start | bytes 786436
  377.3 5.2 copy-start.15
  377.3 5.2 copy-start.22
  377.3 5.7 copy-start.31
  377.3 5.7 copy-start.40
  377.3 5.7 copy-start.55
  378.5 6.6 %copy-start.19 = (f32[128,256]{1,0:T(8,128)}, f32[128,256]{1,0:T(8,128)S(1)}, u32[]{:S(2)}) copy-start(f32[128,256]{1,0:T(8,128)S(1)} %fusion.131) | copy-start | bytes 393220
  380.9 4.3 copy-start.28
  383.0 4.4 copy-start.41
  484.0 9.2 %copy-start.39 = (f32[256,256]{1,0:T(8,128)S(1)}, f32[256,256]{1,0:T(8,128)}, u32[]{:S(2)}) copy-start(f32[256,256]{1,0:T(8,128)} %get-tuple-element.116) | copy-start | bytes 786436
  551.2 36.2 %copy-start.16 = (f32[128,256]{1,0:T(8,128)S(1)}, f32[128,256]{1,0:T(8,128)}, u32[]{:S(2)}) copy-start(f32[128,256]{1,0:T(8,128)} %copy-done.14) | copy-start | bytes 393220
  551.2 36.2 %copy-start.23 = (f32[128,256]{1,0:T(8,128)S(1)}, f32[128,256]{1,0:T(8,128)}, u32[]{:S(2)}) copy-start(f32[128,256]{1,0:T(8,128)} %copy-done.21) | copy-start | bytes 393220
  584.9 6.1 copy-start.9
  588.9 4.7 copy-start.6
  588.9 4.7 copy-start.11
  600.4 5.0 copy-start.18
  (38 other events, 76.9 us)
Sparse Core Ops, SparseCore 0:
  16.1 150.8 all-reduce.3
where the time goes:
time: 627 us; the launch traced here: 618 us
  other arithmetic  273 us (44%)
  waiting for transfers between devices  149 us (24%)
  local copies, waits for them, and re-layouts  92.4 us (15%)
  matrix products  79.7 us (13%)
  between operations  22.7 us (4%)
    another operation x27, other arithmetic, on_device(): lower = jnp.linalg.cholesky(pivot_gram + shift * identity)  159 us
    psum x1, waiting for transfers between devices, on_device(): all_points, all_factor = lax.psum((all_points, all_factor), ('rows', 'sub'))  149 us
    another operation x9, other arithmetic, on_device(): lax.linalg.triangular_solve(lower, identity, left_side=True, lower=True)  88.9 us
    another operation x29, local copies, waits for them, and re-layouts, on_device(): lax.linalg.triangular_solve(lower, identity, left_side=True, lower=True)  33.5 us
    dot_general x14, matrix products, gauss_kernel(): inner = jnp.dot(left, right.T, preferred_element_type=jnp.float32)  13 us
    gather x4, local copies, waits for them, and re-layouts, gershgorin(): jnp.diagonal(pivot_gram)  12.8 us
    another operation x12, matrix products, on_device(): lax.linalg.triangular_solve(lower, identity, left_side=True, lower=True)  12.8 us
  transfers between devices with their start and end apart: 1, of which 1 were waited for; matrix products, arithmetic and copies ran while one was open for 0% of the time, Pallas kernels for 0%

commit v1 on v0

--- a/solution.py
+++ b/solution.py
@@ -39,7 +39,7 @@
         select_all.astype(jnp.bfloat16), embeddings, preferred_element_type=jnp.float32
     )
     all_factor = jnp.dot(select_all, factor, precision=lax.Precision.HIGHEST)
-    all_points, all_factor = lax.psum((all_points, all_factor), ("rows", "sub"))
+    all_points, all_factor = lax.psum(lax.psum((all_points, all_factor), "sub"), "rows")
     for block in range(blocks):
         point_rows = all_points[block * pivots : (block + 1) * pivots]
         factor_rows = jnp.concatenate(

time: 627 us -> 771 us (1.23)
  waiting for transfers between devices: 149 us -> 292 us
    psum x1 -> x2, waiting for transfers between devices: 149 us -> 291 us  [the longest x1 186 us: on_device(): lax.psum(lax.psum((all_points, all_factor), 'sub'), 'rows')]
  transfers between devices with their start and end apart: 1 -> 2, of which waited for: 1 -> 2; matrix products, arithmetic and copies ran while one was open for 0% -> 0% of each run, Pallas kernels for 0% -> 0%
where the time goes in v1:
time: 771 us; the launch traced here: 762 us
  waiting for transfers between devices  292 us (38%)
  other arithmetic  273 us (35%)
  local copies, waits for them, and re-layouts  92.7 us (12%)
  matrix products  81.4 us (11%)
  between operations  23 us (3%)
    psum x1, waiting for transfers between devices, on_device(): lax.psum(lax.psum((all_points, all_factor), 'sub'), 'rows')  186 us
    another operation x27, other arithmetic, on_device(): lower = jnp.linalg.cholesky(pivot_gram + shift * identity)  159 us
    psum x1, waiting for transfers between devices, on_device(): lax.psum((all_points, all_factor), 'sub')  105 us
    another operation x9, other arithmetic, on_device(): lax.linalg.triangular_solve(lower, identity, left_side=True, lower=True)  88.9 us
    another operation x29, local copies, waits for them, and re-layouts, on_device(): lax.linalg.triangular_solve(lower, identity, left_side=True, lower=True)  34 us
  transfers between devices with their start and end apart: 2, of which 2 were waited for; matrix products, arithmetic and copies ran while one was open for 0% of the time, Pallas kernels for 0%

profile of v1, /device:TPU:0, one launch (start us, length us, event | category | flops | bytes accessed | tf_op | source)
XLA Modules:
  0.0 761.7 jit_solution(14886337381846163552)
XLA Ops:
  8.6 3.9 fusion.62
  16.0 105.4 %all-reduce.8.cloned.1.call-done = (f32[1024,768]{1,0:T(8,128)}, f32[1024,512]{1,0:T(8,128)}) async-done(((f32[1024,768]{1,0:T(8,128)}, f32[1024,512]{1,0:T(8,128)}), (f32[1024,768]{1,0:T(8,128)}, f32[1024,512]{1,0:T(8,128)})) %all-reduce.8.cloned.1.call-update) | async-done | bytes 5242896 | tf_op jit(solution)/shard_map/psum | solution.py:42
  123.0 186.1 %all-reduce.6.cloned.1.call-done = (f32[1024,768]{1,0:T(8,128)}, f32[1024,512]{1,0:T(8,128)}) async-done(((f32[1024,768]{1,0:T(8,128)}, f32[1024,512]{1,0:T(8,128)}), (f32[1024,768]{1,0:T(8,128)}, f32[1024,512]{1,0:T(8,128)})) %all-reduce.6.cloned.1.call-update) | async-done | bytes 5242896 | tf_op jit(solution)/shard_map/psum | solution.py:42
  340.0 11.7 %cholesky.214 = f32[128,128]{1,0:T(8,128)S(1)} custom-call(f32[128,128]{1,0:T(8,128)S(1)} %copy.79), custom_call_target="Cholesky" | custom-call | tf_op jit(solution)/shard_map/jit(cholesky)/cholesky | solution.py:58
  354.3 11.3 %custom-call.25 = f32[1,128,128]{1,2,0:T(8,128)} custom-call(f32[1,128,128]{2,1,0:T(8,128)} %get-tuple-element.116), custom_call_target="InvertDiagBlocksLowerTriangular" | custom-call | tf_op jit(solution)/shard_map/jit(cholesky)/cholesky | solution.py:58
  370.1 13.2 %cholesky.231 = f32[128,128]{1,0:T(8,128)} custom-call(f32[128,128]{1,0:T(8,128)} %copy.81), custom_call_target="Cholesky" | custom-call | tf_op jit(solution)/shard_map/jit(cholesky)/cholesky | solution.py:58
  389.7 6.5 while.8
  396.2 21.3 %custom-call.26 = f32[2,128,128]{1,2,0:T(8,128)} custom-call(f32[2,128,128]{2,1,0:T(8,128)} %get-tuple-element.30), custom_call_target="InvertDiagBlocksLowerTriangular" | custom-call | tf_op jit(solution)/shard_map/triangular_solve/custom-call.0 | solution.py:59
  440.4 11.7 %cholesky.248 = f32[128,128]{1,0:T(8,128)S(1)} custom-call(f32[128,128]{1,0:T(8,128)S(1)} %copy.92), custom_call_target="Cholesky" | custom-call | tf_op jit(solution)/shard_map/jit(cholesky)/cholesky | solution.py:58
  454.8 11.3 %custom-call.27 = f32[1,128,128]{1,2,0:T(8,128)} custom-call(f32[1,128,128]{2,1,0:T(8,128)} %get-tuple-element.112), custom_call_target="InvertDiagBlocksLowerTriangular" | custom-call | tf_op jit(solution)/shard_map/jit(cholesky)/cholesky | solution.py:58
  470.6 13.2 %cholesky.265 = f32[128,128]{1,0:T(8,128)} custom-call(f32[128,128]{1,0:T(8,128)} %copy.94), custom_call_target="Cholesky" | custom-call | tf_op jit(solution)/shard_map/jit(cholesky)/cholesky | solution.py:58
  489.5 8.6 %while.9 = (s32[]{:T(128)}, f32[256,256]{1,0:T(8,128)}, s32[2,2]{1,0:T(2,128)}, f32[2,128,128]{2,1,0:T(8,128)}, s32[]{:T(128)}) while((s32[]{:T(128)}, f32[256,256]{1,0:T(8,128)}, s32[2,2]{1,0:T(2,128)}, f32[2,128,128]{2,1,0:T(8,128)}, s32[]{:T(128)}) %tuple.121), condition=%wide.while_cond.clone, body=%wide.while_body.clone.sunk | while | flops 2 | bytes 132705 | solution.py:59
  498.2 21.3 %custom-call.28 = f32[2,128,128]{1,2,0:T(8,128)} custom-call(f32[2,128,128]{2,1,0:T(8,128)} %get-tuple-element.31), custom_call_target="InvertDiagBlocksLowerTriangular" | custom-call | tf_op jit(solution)/shard_map/triangular_solve/custom-call.0 | solution.py:59
  548.5 11.7 %cholesky.282 = f32[128,128]{1,0:T(8,128)S(1)} custom-call(f32[128,128]{1,0:T(8,128)S(1)} %cholesky.352), custom_call_target="Cholesky" | custom-call | tf_op jit(solution)/shard_map/jit(cholesky)/cholesky | solution.py:58
  562.9 11.3 %custom-call.29 = f32[1,128,128]{1,2,0:T(8,128)} custom-call(f32[1,128,128]{2,1,0:T(8,128)} %get-tuple-element.108), custom_call_target="InvertDiagBlocksLowerTriangular" | custom-call | tf_op jit(solution)/shard_map/jit(cholesky)/cholesky | solution.py:58
  577.0 13.2 %cholesky.299 = f32[128,128]{1,0:T(8,128)} custom-call(f32[128,128]{1,0:T(8,128)} %convolution_subtract_fusion.10), custom_call_target="Cholesky" | custom-call | tf_op jit(solution)/shard_map/jit(cholesky)/cholesky | solution.py:58
  595.9 6.5 while.10
  602.4 21.1 %custom-call.30 = f32[2,128,128]{1,2,0:T(8,128)} custom-call(f32[2,128,128]{2,1,0:T(8,128)} %get-tuple-element.32), custom_call_target="InvertDiagBlocksLowerTriangular" | custom-call | tf_op jit(solution)/shard_map/triangular_solve/custom-call.0 | solution.py:59
  648.1 11.7 %cholesky.316 = f32[128,128]{1,0:T(8,128)S(1)} custom-call(f32[128,128]{1,0:T(8,128)S(1)} %cholesky.355), custom_call_target="Cholesky" | custom-call | tf_op jit(solution)/shard_map/jit(cholesky)/cholesky | solution.py:58
  661.9 11.3 %custom-call.31 = f32[1,128,128]{1,2,0:T(8,128)} custom-call(f32[1,128,128]{2,1,0:T(8,128)} %get-tuple-element.104), custom_call_target="InvertDiagBlocksLowerTriangular" | custom-call | tf_op jit(solution)/shard_map/jit(cholesky)/cholesky | solution.py:58
  676.0 13.2 %cholesky.333 = f32[128,128]{1,0:T(8,128)} custom-call(f32[128,128]{1,0:T(8,128)} %convolution_subtract_fusion.9), custom_call_target="Cholesky" | custom-call | tf_op jit(solution)/shard_map/jit(cholesky)/cholesky | solution.py:58
  694.2 8.4 %while.11 = (s32[]{:T(128)}, f32[256,256]{1,0:T(8,128)}, s32[2,2]{1,0:T(2,128)}, f32[2,128,128]{2,1,0:T(8,128)}, s32[]{:T(128)}) while((s32[]{:T(128)}, f32[256,256]{1,0:T(8,128)}, s32[2,2]{1,0:T(2,128)}, f32[2,128,128]{2,1,0:T(8,128)}, s32[]{:T(128)}) %tuple.123), condition=%wide.while_cond.clone.2, body=%wide.while_body.clone.2.sunk | while | flops 2 | bytes 132705 | solution.py:59
  702.7 21.3 %custom-call.32 = f32[2,128,128]{1,2,0:T(8,128)} custom-call(f32[2,128,128]{2,1,0:T(8,128)} %get-tuple-element.33), custom_call_target="InvertDiagBlocksLowerTriangular" | custom-call | tf_op jit(solution)/shard_map/triangular_solve/custom-call.0 | solution.py:59
  746.7 3.7 fusion
  (305 shorter events, 210.0 us)
Async XLA Ops:
  7.2 114.2 %all-reduce.8.cloned.1.call-start = ((), (), s32[]{:S(2)}) async-start(), calls=%async_computation.1 | async-start | bytes 10485760 | tf_op jit(solution)/shard_map/psum | solution.py:42
  16.0 293.2 %all-reduce.6.cloned.1.call-start = ((), (), s32[]{:S(2)}) async-start(), calls=%async_computation | async-start | bytes 10485760 | tf_op jit(solution)/shard_map/psum | solution.py:42
  312.0 5.9 copy-start.10
  312.0 10.3 %copy-start.11 = (bf16[256,768]{1,0:T(8,128)(2,1)}, bf16[256,768]{1,0:T(8,128)(2,1)S(1)}, u32[]{:S(2)}) copy-start(bf16[256,768]{1,0:T(8,128)(2,1)S(1)} %get-tuple-element.95) | copy-start | bytes 1179652
  312.3 10.0 %copy-start.61 = (f32[256]{0:T(256)}, f32[256]{0:T(256)S(1)}, u32[]{:S(2)}) copy-start(f32[256]{0:T(256)S(1)} %get-tuple-element.39) | copy-start | bytes 3076
  312.6 12.0 %copy-start.27 = (f32[256,256]{0,1:T(8,128)}, f32[256,256]{0,1:T(8,128)S(1)}, u32[]{:S(2)}) copy-start(f32[256,256]{0,1:T(8,128)S(1)} %convolution_multiply_fusion.13) | copy-start | bytes 786436
  417.5 4.3 copy-start.58
  418.7 4.8 copy-start.13
  421.8 6.2 copy-start.26
  489.5 35.6 %copy-start.8 = (f32[256,256]{1,0:T(8,128)S(1)}, f32[256,256]{1,0:T(8,128)}, u32[]{:S(2)}) copy-start(f32[256,256]{1,0:T(8,128)} %copy-done.7) | copy-start | bytes 786436
  519.4 5.2 copy-start.14
  519.4 5.2 copy-start.23
  519.4 5.7 copy-start.32
  519.4 5.7 copy-start.41
  519.4 5.7 copy-start.59
  520.7 6.6 copy-start.20
  523.0 4.3 copy-start.30
  525.1 4.4 copy-start.43
  626.7 9.2 %copy-start.40 = (f32[256,256]{1,0:T(8,128)S(1)}, f32[256,256]{1,0:T(8,128)}, u32[]{:S(2)}) copy-start(f32[256,256]{1,0:T(8,128)} %get-tuple-element.118) | copy-start | bytes 786436
  694.2 36.4 %copy-start.15 = (f32[128,256]{1,0:T(8,128)S(1)}, f32[128,256]{1,0:T(8,128)}, u32[]{:S(2)}) copy-start(f32[128,256]{1,0:T(8,128)} %copy-done.13) | copy-start | bytes 393220
  694.2 36.4 %copy-start.24 = (f32[128,256]{1,0:T(8,128)S(1)}, f32[128,256]{1,0:T(8,128)}, u32[]{:S(2)}) copy-start(f32[128,256]{1,0:T(8,128)} %copy-done.22) | copy-start | bytes 393220
  728.1 6.1 copy-start.9
  732.1 4.6 copy-start.6
  738.9 4.5 copy-start.17
  (43 other events, 91.3 us)
Sparse Core Ops, SparseCore 0:
  16.1 105.2 all-reduce.7
  125.2 183.9 all-reduce.5
